TPU v7x, 32 devices: a whole 2x2x4 slice. The times are simulated.
32 devices in a mesh: heads: 4 (over y, core), tok: 8 (over z, x).
Axes of the slice: x: 2, y: 2, z: 4, core: 2. Of those that a mesh axis runs over, the one named last changes fastest.
Arguments:
- video_q: bfloat16 [8192, 2048], P('tok', 'heads'), as said below
- video_k: bfloat16 [8192, 2048], P('tok', 'heads'), as said below
- video_v: bfloat16 [8192, 2048], P('tok', 'heads'), may hold values from -6 to 6
- audio_q: bfloat16 [512, 2048], P('tok', 'heads'), as said below
- audio_k: bfloat16 [512, 2048], P('tok', 'heads'), as said below
- audio_v: bfloat16 [512, 2048], P('tok', 'heads'), may hold values from -6 to 6
- video_q_gain: float32 [2048], P('heads'), may hold values from 0.1 to 1.9
- audio_k_gain: float32 [2048], P('heads'), may hold values from 0.1 to 1.9
- audio_q_gain: float32 [2048], P('heads'), may hold values from 0.1 to 1.9
- video_k_gain: float32 [2048], P('heads'), may hold values from 0.1 to 1.9
Outputs:
- video_out: bfloat16 [8192, 2048], P('tok', 'heads')
- audio_out: bfloat16 [512, 2048], P('tok', 'heads')
Inputs may be any that keep to these rules, and one draw needn't show every extreme that they name: `video_q`: no row is zero. `video_k`: no row is zero. `audio_q`: no row is zero. `audio_k`: no row is zero.
All inputs are finite; a program needn't handle non-finite values.
Results may differ from a plain program's by a relative error of at most 0.012.
The roundings to bfloat16 on the way count: a program that leaves them out, or rounds other values in their place, can miss the bound.
Values may be sent and summed in bfloat16 or wider, within the bound.
No kernel may reach another device: no remote copies, remote signals or barrier semaphores. Data moves between devices by JAX's collectives and lax.ppermute only.
A program may use at most 64 MiB of HBM per device.

v0:
```python
import math
import jax
import jax.numpy as jnp
from jax import lax
from jax.sharding import PartitionSpec as P

HEADS = 32
HD = 64
EPS = 1e-06


def squares(rows):
    values = rows.astype(jnp.float32)
    return jnp.sum(values * values, axis=1)


def normalize(rows, summed, gain):
    scaled = lax.rsqrt(summed / (HEADS * HD) + EPS)[:, None]
    return (rows.astype(jnp.float32) * scaled * gain).astype(jnp.bfloat16)


def body(
    video_q,
    video_k,
    video_v,
    audio_q,
    audio_k,
    audio_v,
    video_q_gain,
    audio_k_gain,
    audio_q_gain,
    video_k_gain,
):
    factor = HD ** (-0.5)
    tok_rows = video_q.shape[0]
    aud_rows = audio_q.shape[0]
    local_width = video_q.shape[1]
    local_heads = local_width // HD
    sum_vq, sum_ak, sum_aq, sum_vk = lax.psum(
        (squares(video_q), squares(audio_k), squares(audio_q), squares(video_k)), "heads"
    )
    query_v = normalize(video_q, sum_vq, video_q_gain)
    key_a = normalize(audio_k, sum_ak, audio_k_gain)
    query_a = normalize(audio_q, sum_aq, audio_q_gain)
    key_v = normalize(video_k, sum_vk, video_k_gain)
    key_all, value_all, query_all = (
        lax.all_gather(key_a, "tok", axis=0, tiled=True),
        lax.all_gather(audio_v, "tok", axis=0, tiled=True),
        lax.all_gather(query_a, "tok", axis=0, tiled=True),
    )
    audio_total = key_all.shape[0]
    key_heads = key_all.reshape(audio_total, local_heads, HD)
    value_heads = value_all.reshape(audio_total, local_heads, HD)
    block = math.gcd(tok_rows, 512)
    count = tok_rows // block

    def first(pair):
        query, value = pair
        scores = (
            jnp.einsum(
                "qhd,khd->hqk",
                query.reshape(block, local_heads, HD),
                key_heads,
                preferred_element_type=jnp.float32,
            )
            * factor
        )
        top = jnp.max(scores, axis=-1, keepdims=True)
        expo = jnp.exp(scores - top)
        total = jnp.sum(expo, axis=-1)
        weights = expo.astype(jnp.bfloat16)
        mixed = (
            jnp.einsum("hqk,khd->qhd", weights, value_heads, preferred_element_type=jnp.float32)
            / jnp.transpose(total)[:, :, None]
        )
        return (value.astype(jnp.float32) + mixed.reshape(block, local_width)).astype(jnp.bfloat16)

    video_out = lax.map(
        first,
        (query_v.reshape(count, block, local_width), video_v.reshape(count, block, local_width)),
    ).reshape(tok_rows, local_width)
    key_local = key_v.reshape(tok_rows, local_heads, HD)
    value_local = video_out.reshape(tok_rows, local_heads, HD)
    rows_block = math.gcd(audio_total, 512)
    rows_count = audio_total // rows_block

    def second(query):
        scores = (
            jnp.einsum(
                "qhd,khd->hqk",
                query.reshape(rows_block, local_heads, HD),
                key_local,
                preferred_element_type=jnp.float32,
            )
            * factor
        )
        top = jnp.max(scores, axis=-1)
        expo = jnp.exp(scores - top[:, :, None])
        total = jnp.sum(expo, axis=-1)
        weights = expo.astype(jnp.bfloat16)
        part = jnp.einsum("hqk,khd->qhd", weights, value_local, preferred_element_type=jnp.float32)
        return (part, jnp.transpose(top), jnp.transpose(total))

    partial_value, tops, totals = lax.map(
        second, query_all.reshape(rows_count, rows_block, local_width)
    )
    partial_value = partial_value.reshape(audio_total, local_heads, HD)
    tops = tops.reshape(audio_total, local_heads)
    totals = totals.reshape(audio_total, local_heads)
    got_part, got_top, got_total = (
        lax.all_to_all(partial_value, "tok", split_axis=0, concat_axis=0, tiled=True),
        lax.all_to_all(tops, "tok", split_axis=0, concat_axis=0, tiled=True),
        lax.all_to_all(totals, "tok", split_axis=0, concat_axis=0, tiled=True),
    )
    senders = got_part.shape[0] // aud_rows
    got_part = got_part.reshape(senders, aud_rows, local_heads, HD)
    got_top = got_top.reshape(senders, aud_rows, local_heads)
    got_total = got_total.reshape(senders, aud_rows, local_heads)
    highest = jnp.max(got_top, axis=0)
    scale_rows = jnp.exp(got_top - highest[None])
    summed = jnp.sum(got_part * scale_rows[:, :, :, None], axis=0)
    denominator = jnp.sum(got_total * scale_rows, axis=0)
    audio_out = (
        (summed / denominator[:, :, None]).reshape(aud_rows, local_width).astype(jnp.bfloat16)
    )
    return (video_out, audio_out)


def solution(mesh):
    return jax.shard_map(
        body,
        mesh=mesh,
        in_specs=(
            P("tok", "heads"),
            P("tok", "heads"),
            P("tok", "heads"),
            P("tok", "heads"),
            P("tok", "heads"),
            P("tok", "heads"),
            P("heads"),
            P("heads"),
            P("heads"),
            P("heads"),
        ),
        out_specs=(P("tok", "heads"), P("tok", "heads")),
        check_vma=False,
    )
```

profile of v0, /device:TPU:0, one launch (start us, length us, event | category | flops | bytes accessed | tf_op | source)
XLA Modules:
  0.0 202.1 jit_solution(3499566334324354814)
XLA Ops:
  2.6 1.5 fusion.18
  4.1 1.5 copy.49
  5.8 8.7 %all-reduce = (f32[1024]{0:T(1024)S(1)}, f32[64]{0:T(128)S(1)}, f32[64]{0:T(128)S(1)}, f32[1024]{0:T(1024)S(1)}) all-reduce(f32[1024]{0:T(1024)S(1)} %fusion.18, f32[64]{0:T(128)S(1)} %fusion.27, f32[64]{0:T(128)S(1)} %fusion.30, f32[1024]{0:T(1024)S(1)} %fusion.21), channel_id=1, replica_groups=mesh['heads'=4,'tok'=8] {'heads'}, use_global_device_ids=true, to_apply=%region_1.0 | all-reduce | flops 2176 | bytes 17408 | tf_op jit(solution)/shard_map/psum | solution.py:39
  15.5 32.0 %all_gather.11 = bf16[512,512]{1,0:T(8,128)(2,1)S(1)} all-gather(bf16[64,512]{1,0:T(8,128)(2,1)S(1)} %fusion.32), channel_id=1, replica_groups=mesh['heads'=4,'tok'=8] {'tok'}, dimensions={0}, use_global_device_ids=true | all-gather | bytes 589824 | tf_op jit(solution)/shard_map/all_gather | solution.py:49
  48.7 8.1 %multiply_reduce_fusion.1 = (f32[8,512]{1,0:T(8,128)S(1)}, f32[8,512,1024]{2,1,0:T(8,128)}) fusion(bf16[512,8,64]{0,2,1:T(8,128)(2,1)S(1)} %bitcast.64, bf16[1024,8,64]{0,2,1:T(8,128)(2,1)S(1)} %bitcast.63), kind=kOutput, calls=%fused_computation.16 | convolution fusion | flops 545255424 | bytes 18366464 | tf_op jit(solution)/shard_map/while/body/eval_jaxpr/qhd,khd->hqk/dot_general | solution.py:89
  57.6 5.3 %all-to-all-start.1 = ((f32[8,1,512]{2,1,0:T(1,128)}), f32[8,1,512]{2,1,0:T(1,128)S(1)}, u32[]{:S(2)}, u32[]{:S(2)}) async-start(f32[8,1,512]{2,1,0:T(1,128)} %reshape.88), calls=%async_computation.1 | async-start | bytes 32768 | tf_op jit(solution)/shard_map/all_to_all | solution.py:112
  62.9 32.0 %all_gather.10 = bf16[512,512]{1,0:T(8,128)(2,1)S(1)} all-gather(bf16[64,512]{1,0:T(8,128)(2,1)S(1)} %copy-done.6), channel_id=1, replica_groups=mesh['heads'=4,'tok'=8] {'tok'}, dimensions={0}, use_global_device_ids=true | all-gather | bytes 589824 | tf_op jit(solution)/shard_map/all_gather | solution.py:48
  96.0 31.4 %all_gather.9 = bf16[512,512]{1,0:T(8,128)(2,1)S(1)} all-gather(bf16[64,512]{1,0:T(8,128)(2,1)S(1)} %fusion.29), channel_id=1, replica_groups=mesh['heads'=4,'tok'=8] {'tok'}, dimensions={0}, use_global_device_ids=true | all-gather | bytes 589824 | tf_op jit(solution)/shard_map/all_gather | solution.py:47
  127.9 14.4 %while.2 = (s32[]{:T(128)}, bf16[2,512,512]{1,2,0:T(8,128)(2,1)}, bf16[2,512,512]{2,1,0:T(8,128)(2,1)}, bf16[2,512,512]{2,1,0:T(8,128)(2,1)S(1)}, bf16[512,8,64]...) while((s32[]{:T(128)}, bf16[2,512,512]{1,2,0:T(8,128)(2,1)}, ...), condition=%wide.region_7.0_spmd, body=%wide.region_4.7_spmd.sunk | while | flops 554688512 | bytes 44646576 | solution.py:78
  130.8 1.4 fusion.50
  132.2 1.7 fusion.51
  138.0 1.4 fusion.50
  139.4 1.7 fusion.51
  142.3 7.7 %fusion.14 = f32[8,512]{1,0:T(8,128)S(1)} fusion(f32[8,512,1024]{2,1,0:T(8,128)} %get-tuple-element.101, f32[8,512]{1,0:T(8,128)S(1)} %get-tuple-element.100), kind=kLoop, calls=%fused_computation.17 | loop fusion | flops 12578816 | bytes 16809984 | tf_op jit(solution)/shard_map/while/body/eval_jaxpr/reduce_sum | solution.py:99
  152.7 5.6 %all-to-all-start.2 = ((f32[8,1,512]{2,1,0:T(1,128)}), f32[8,1,512]{2,1,0:T(1,128)S(1)}, u32[]{:S(2)}, u32[]{:S(2)}) async-start(f32[8,1,512]{2,1,0:T(1,128)} %reshape.90), calls=%async_computation.2 | async-start | bytes 32768 | tf_op jit(solution)/shard_map/all_to_all | solution.py:113
  158.2 8.2 %fusion.24 = f32[512,8,64]{0,2,1:T(8,128)} fusion(bf16[1024,8,64]{0,2,1:T(8,128)(2,1)S(1)} %reshape_reshape.3, f32[8,512,1024]{2,1,0:T(8,128)} %get-tuple-element.101, f32[8,512]{1,0:T(8,128)S(1)} %get-tuple-element.100), kind=kOutput, calls=%fused_computation.31 | convolution fusion | flops 549453824 | bytes 18890752 | tf_op jit(solution)/shard_map/while/body/eval_jaxpr/hqk,khd->qhd/dot_general | solution.py:101
  166.4 2.0 copy.50
  168.4 2.1 %reshape.86 = f32[8,1,32768]{2,1,0:T(1,128)} reshape(f32[512,8,64]{2,1,0:T(8,128)S(1)} %copy.50) | data formatting | bytes 2097152
  170.6 6.0 %all-to-all-start = ((f32[8,1,32768]{2,1,0:T(1,128)}), f32[8,1,32768]{2,1,0:T(1,128)S(1)}, u32[]{:S(2)}, u32[]{:S(2)}) async-start(f32[8,1,32768]{2,1,0:T(1,128)} %reshape.86), calls=%async_computation | async-start | bytes 2097152 | tf_op jit(solution)/shard_map/all_to_all | solution.py:111
  176.6 1.3 copy.46
  180.0 13.0 %all-to-all-done = f32[8,1,32768]{2,1,0:T(1,128)S(1)} async-done(((f32[8,1,32768]{2,1,0:T(1,128)}), f32[8,1,32768]{2,1,0:T(1,128)S(1)}, u32[]{:S(2)}, u32[]{:S(2)}) %all-to-all-start) | async-done | bytes 1048608 | tf_op jit(solution)/shard_map/all_to_all | solution.py:111
  192.9 3.1 %reduce.1 = f32[8,32768]{1,0:T(8,128)S(1)} reduce(f32[8,1,32768]{2,1,0:T(1,128)S(1)} %all-to-all-done, f32[]{:T(128)} %broadcast.70), dimensions={1}, to_apply=%all_to_all.15.reduce_sub_computation | reduce | bytes 2097156 | tf_op jit(solution)/shard_map/all_to_all | solution.py:111
  196.1 2.2 %reshape.87 = f32[512,8,64]{2,1,0:T(8,128)} reshape(f32[8,32768]{1,0:T(8,128)S(1)} %reduce.1) | data formatting | bytes 2097152
  198.3 2.4 %copy.53 = f32[8,64,8,64]{1,0,3,2:T(8,128)S(1)} copy(f32[8,64,8,64]{3,2,1,0:T(8,128)} %bitcast.61) | data formatting | bytes 2097152 | tf_op jit(solution)/shard_map/reshape | solution.py:116
  (69 shorter events, 20.8 us)
Async XLA Ops:
  48.6 14.2 %copy-start.6 = (bf16[64,512]{1,0:T(8,128)(2,1)S(1)}, bf16[64,512]{1,0:T(8,128)(2,1)}, u32[]{:S(2)}) copy-start(bf16[64,512]{1,0:T(8,128)(2,1)} %param.17) | copy-start | bytes 196612
  48.6 47.2 %copy-start.5 = (bf16[64,512]{1,0:T(8,128)(2,1)S(1)}, bf16[64,512]{1,0:T(8,128)(2,1)}, u32[]{:S(2)}) copy-start(bf16[64,512]{1,0:T(8,128)(2,1)} %param.16) | copy-start | bytes 196612
  48.6 47.2 %copy-start.7 = (f32[512]{0:T(512)S(1)}, f32[512]{0:T(512)}, u32[]{:S(2)}) copy-start(f32[512]{0:T(512)} %param.19) | copy-start | bytes 6148
  48.7 78.9 %copy-start = (bf16[1024,512]{1,0:T(8,128)(2,1)S(1)}, bf16[1024,512]{1,0:T(8,128)(2,1)}, u32[]{:S(2)}) copy-start(bf16[1024,512]{1,0:T(8,128)(2,1)} %param.12) | copy-start | bytes 3145732
  48.7 78.9 %copy-start.8 = (f32[512]{0:T(512)S(1)}, f32[512]{0:T(512)}, u32[]{:S(2)}) copy-start(f32[512]{0:T(512)} %param.18) | copy-start | bytes 6148
  57.6 95.1 %all-to-all-start.1 = ((f32[8,1,512]{2,1,0:T(1,128)}), f32[8,1,512]{2,1,0:T(1,128)S(1)}, u32[]{:S(2)}, u32[]{:S(2)}) async-start(f32[8,1,512]{2,1,0:T(1,128)} %reshape.88), calls=%async_computation.1 | async-start | bytes 32768 | tf_op jit(solution)/shard_map/all_to_all | solution.py:112
  129.5 2.7 %copy-start.4 = (bf16[512,8,64]{0,2,1:T(8,128)(2,1)S(1)}, bf16[512,8,64]{0,2,1:T(8,128)(2,1)}, u32[]{:S(2)}) copy-start(bf16[512,8,64]{0,2,1:T(8,128)(2,1)} %get-tuple-element.168) | copy-start | bytes 1572868 | tf_op jit(solution)/shard_map/while
  130.8 3.1 %copy-start.1 = (bf16[2,512,512]{1,2,0:T(8,128)(2,1)S(1)}, bf16[2,512,512]{1,2,0:T(8,128)(2,1)}, u32[]{:S(2)}) copy-start(bf16[2,512,512]{1,2,0:T(8,128)(2,1)} %get-tuple-element.157) | copy-start | bytes 3145732 | tf_op jit(solution)/shard_map/while
  134.1 1.0 copy-start.2
  136.7 2.7 %copy-start.4 = (bf16[512,8,64]{0,2,1:T(8,128)(2,1)S(1)}, bf16[512,8,64]{0,2,1:T(8,128)(2,1)}, u32[]{:S(2)}) copy-start(bf16[512,8,64]{0,2,1:T(8,128)(2,1)} %get-tuple-element.168) | copy-start | bytes 1572868 | tf_op jit(solution)/shard_map/while
  138.0 3.1 %copy-start.1 = (bf16[2,512,512]{1,2,0:T(8,128)(2,1)S(1)}, bf16[2,512,512]{1,2,0:T(8,128)(2,1)}, u32[]{:S(2)}) copy-start(bf16[2,512,512]{1,2,0:T(8,128)(2,1)} %get-tuple-element.157) | copy-start | bytes 3145732 | tf_op jit(solution)/shard_map/while
  141.3 1.0 copy-start.2
  142.3 7.7 %copy-start.3 = (bf16[2,512,512]{1,2,0:T(8,128)(2,1)S(1)}, bf16[2,512,512]{1,2,0:T(8,128)(2,1)}, u32[]{:S(2)}) copy-start(bf16[2,512,512]{1,2,0:T(8,128)(2,1)} %get-tuple-element.55) | copy-start | bytes 3145732
  152.7 17.9 %all-to-all-start.2 = ((f32[8,1,512]{2,1,0:T(1,128)}), f32[8,1,512]{2,1,0:T(1,128)S(1)}, u32[]{:S(2)}, u32[]{:S(2)}) async-start(f32[8,1,512]{2,1,0:T(1,128)} %reshape.90), calls=%async_computation.2 | async-start | bytes 32768 | tf_op jit(solution)/shard_map/all_to_all | solution.py:113
  170.6 22.4 %all-to-all-start = ((f32[8,1,32768]{2,1,0:T(1,128)}), f32[8,1,32768]{2,1,0:T(1,128)S(1)}, u32[]{:S(2)}, u32[]{:S(2)}) async-start(f32[8,1,32768]{2,1,0:T(1,128)} %reshape.86), calls=%async_computation | async-start | bytes 2097152 | tf_op jit(solution)/shard_map/all_to_all | solution.py:111
where the time goes:
time: 203 us; the launch traced here: 202 us
  blocking collectives  104 us (51%)
  local copies, waits for them, and re-layouts  22.8 us (11%)
  matrix products  22.3 us (11%)
  other arithmetic  22 us (11%)
  starting transfers between devices  16.8 us (8%)
  waiting for transfers between devices  13 us (6%)
    all_gather x1, blocking collectives, body(): lax.all_gather(audio_v, 'tok', axis=0, tiled=True)  32 us
    all_gather x1, blocking collectives, body(): lax.all_gather(query_a, 'tok', axis=0, tiled=True)  32 us
    all_gather x1, blocking collectives, body(): lax.all_gather(key_a, 'tok', axis=0, tiled=True)  31.4 us
    all_to_all x1, waiting for transfers between devices, body(): lax.all_to_all(partial_value, 'tok', split_axis=0, concat_axis=0, tiled=T...  13 us
    psum x1, blocking collectives, body(): lax.psum((squares(video_q), squares(audio_k), squares(audio_q), squares(v...  8.72 us
    dot_general x1, matrix products, second(): jnp.einsum('hqk,khd->qhd', weights, value_local, preferred_element_type=j...  8.17 us
    unnamed x20, local copies, waits for them, and re-layouts  8.12 us
    dot_general x1, matrix products, second(): jnp.einsum('qhd,khd->hqk', query.reshape(rows_block, local_heads, HD), ke...  8.11 us
  transfers between devices with their start and end apart: 3, of which 1 were waited for; matrix products, arithmetic and copies ran while one was open for 20% of the time, Pallas kernels for 0%

commit v1 on v0

--- a/solution.py
+++ b/solution.py
@@ -7,6 +7,18 @@
 HEADS = 32
 HD = 64
 EPS = 1e-06
+
+
+def collect(x, axis, dim):
+    ways, here = (lax.axis_size(axis), lax.axis_index(axis))
+    grown, reach = (x, 1)
+    while reach < ways:
+        theirs = lax.ppermute(grown, axis, [(d, d ^ reach) for d in range(ways)])
+        mine_first = jnp.concatenate([grown, theirs], axis=dim)
+        theirs_first = jnp.concatenate([theirs, grown], axis=dim)
+        grown = jnp.where(here & reach == 0, mine_first, theirs_first)
+        reach = 2 * reach
+    return grown
 
 
 def squares(rows):
@@ -46,7 +58,7 @@
     key_all, value_all, query_all = (
         lax.all_gather(key_a, "tok", axis=0, tiled=True),
         lax.all_gather(audio_v, "tok", axis=0, tiled=True),
-        lax.all_gather(query_a, "tok", axis=0, tiled=True),
+        collect(query_a, "tok", 0),
     )
     audio_total = key_all.shape[0]
     key_heads = key_all.reshape(audio_total, local_heads, HD)

time: 203 us -> 184 us (0.906)
  blocking collectives: 104 us -> 72.1 us
  other arithmetic: 22 us -> 25.8 us
  waiting for transfers between devices: 13 us -> 16.5 us
  local copies, waits for them, and re-layouts: 22.8 us -> 25.5 us
  starting transfers between devices: 16.8 us -> 19.3 us
    all_gather x1 -> x0, blocking collectives: 32 us -> none  [body(): lax.all_gather(query_a, 'tok', axis=0, tiled=True)]
    ppermute x0 -> x3, waiting for transfers between devices: none -> 3.48 us  [collect(): theirs = lax.ppermute(grown, axis, [(d, d ^ reach) for d in range(ways)])]
    ppermute x0 -> x3, starting transfers between devices: none -> 2.73 us  [collect(): theirs = lax.ppermute(grown, axis, [(d, d ^ reach) for d in range(ways)])]
    convert_element_type x4, other arithmetic: 2.26 us -> 4.77 us  [normalize(): return (rows.astype(jnp.float32) * scaled * gain).astype(jnp.bfloat16)]
    select_n x0 -> x4, other arithmetic: none -> 2.18 us  [collect(): grown = jnp.where(here & reach == 0, mine_first, theirs_first)]
    unnamed x20 -> x17, local copies, waits for them, and re-layouts: 8.12 us -> 9.69 us
  transfers between devices with their start and end apart: 3 -> 6, of which waited for: 1 -> 2; matrix products, arithmetic and copies ran while one was open for 20% -> 25% of each run, Pallas kernels for 0% -> 0%
where the time goes in v1:
time: 184 us
  blocking collectives  72.1 us (39%)
  other arithmetic  25.8 us (14%)
  local copies, waits for them, and re-layouts  25.5 us (14%)
  matrix products  23.4 us (13%)
  starting transfers between devices  19.3 us (10%)
  waiting for transfers between devices  16.5 us (9%)
    all_gather x1, blocking collectives, body(): lax.all_gather(audio_v, 'tok', axis=0, tiled=True)  32 us
    all_gather x1, blocking collectives, body(): lax.all_gather(key_a, 'tok', axis=0, tiled=True)  31.4 us
    all_to_all x1, waiting for transfers between devices, body(): lax.all_to_all(partial_value, 'tok', split_axis=0, concat_axis=0, tiled=T...  13 us
    unnamed x17, local copies, waits for them, and re-layouts  9.69 us
    dot_general x1, matrix products, second(): jnp.einsum('qhd,khd->hqk', query.reshape(rows_block, local_heads, HD), ke...  9.14 us
    psum x1, blocking collectives, body(): lax.psum((squares(video_q), squares(audio_k), squares(audio_q), squares(v...  8.72 us
    dot_general x1, matrix products, second(): jnp.einsum('hqk,khd->qhd', weights, value_local, preferred_element_type=j...  8.19 us
    reduce_sum x1, other arithmetic, second(): total = jnp.sum(expo, axis=-1)  7.63 us
  transfers between devices with their start and end apart: 6, of which 2 were waited for; matrix products, arithmetic and copies ran while one was open for 25% of the time, Pallas kernels for 0%

profile of v1, /device:TPU:0, one launch (start us, length us, event | category | flops | bytes accessed | tf_op | source)
XLA Modules:
  0.0 183.6 jit_solution(17057252333425508569)
XLA Ops:
  1.6 1.5 fusion.18
  5.9 8.7 %all-reduce = (f32[1024]{0:T(1024)S(1)}, f32[64]{0:T(128)S(1)}, f32[1024]{0:T(1024)S(1)}, f32[64]{0:T(128)S(1)}) all-reduce(f32[1024]{0:T(1024)S(1)} %fusion.18, f32[64]{0:T(128)S(1)} %fusion.37, f32[1024]{0:T(1024)S(1)} %fusion.21, f32[64]{0:T(128)S(1)} %fusion.34), channel_id=1, replica_groups=mesh['heads'=4,'tok'=8] {'heads'}, use_global_device_ids=true, to_apply=%region_1.0 | all-reduce | flops 2176 | bytes 17408 | tf_op jit(solution)/shard_map/psum | solution.py:51
  15.5 1.6 collective-permute-start
  17.0 32.0 %all_gather.7 = bf16[512,512]{1,0:T(8,128)(2,1)S(1)} all-gather(bf16[64,512]{1,0:T(8,128)(2,1)} %param.17), channel_id=1, replica_groups=mesh['heads'=4,'tok'=8] {'tok'}, dimensions={0}, use_global_device_ids=true | all-gather | bytes 589824 | tf_op jit(solution)/shard_map/all_gather | solution.py:60
  50.0 1.5 fusion.20
  51.5 31.4 %all_gather.6 = bf16[512,512]{1,0:T(8,128)(2,1)S(1)} all-gather(bf16[64,512]{1,0:T(8,128)(2,1)S(1)} %fusion.39), channel_id=1, replica_groups=mesh['heads'=4,'tok'=8] {'tok'}, dimensions={0}, use_global_device_ids=true | all-gather | bytes 589824 | tf_op jit(solution)/shard_map/all_gather | solution.py:59
  85.1 14.4 %while.2 = (s32[]{:T(128)}, bf16[2,512,512]{1,2,0:T(8,128)(2,1)}, bf16[2,512,512]{2,1,0:T(8,128)(2,1)}, bf16[2,512,512]{2,1,0:T(8,128)(2,1)S(1)}, bf16[512,8,64]...) while((s32[]{:T(128)}, bf16[2,512,512]{1,2,0:T(8,128)(2,1)}, ...), condition=%wide.region_7.0_spmd, body=%wide.region_4.7_spmd.sunk | while | flops 554688512 | bytes 44646576 | solution.py:90
  89.4 1.7 fusion.58
  96.6 1.7 fusion.58
  101.4 1.5 fusion.23
  102.9 2.3 %copy.54 = bf16[2,512,512]{1,0,2:T(2,128)(2,1)S(1)} copy(bf16[2,512,512]{1,2,0:T(8,128)(2,1)} %get-tuple-element.55) | data formatting | bytes 2097152 | tf_op jit(solution)/shard_map/while | solution.py:90
  107.2 3.5 %collective-permute-done.2 = bf16[256,512]{0,1:T(8,128)(2,1)} collective-permute-done((bf16[256,512]{0,1:T(8,128)(2,1)}, bf16[256,512]{0,1:T(8,128)(2,1)}, u32[]{:S(2)}, u32[]{:S(2)}) %collective-permute-start.2) | collective-permute-done | bytes 262176 | tf_op jit(solution)/shard_map/ppermute | solution.py:16
  110.7 9.1 %multiply_reduce_fusion.1 = (f32[8,512]{1,0:T(8,128)S(1)}, f32[8,512,1024]{2,1,0:T(8,128)}) fusion(bf16[1024,8,64]{0,2,1:T(8,128)(2,1)S(1)} %bitcast.65, bf16[256,8,64]{0,2,1:T(8,128)(2,1)} %bitcast.12, bf16[256,8,64]{0,2,1:T(8,128)(2,1)S(1)} %maximum_select_fusion.2, pred[]{:T(512)S(6)} %eq.9), kind=kOutput, calls=%fused_computation.16 | convolution fusion | flops 547614720 | bytes 18366464 | tf_op jit(solution)/shard_map/while/body/eval_jaxpr/qhd,khd->hqk/dot_general | solution.py:101
  120.6 4.6 %all-to-all-start.1 = ((f32[8,1,512]{2,1,0:T(1,128)}), f32[8,1,512]{2,1,0:T(1,128)S(1)}, u32[]{:S(2)}, u32[]{:S(2)}) async-start(f32[8,1,512]{2,1,0:T(1,128)} %reshape.97), calls=%async_computation.1 | async-start | bytes 32768 | tf_op jit(solution)/shard_map/all_to_all | solution.py:124
  125.2 7.6 %fusion.14 = f32[8,512]{1,0:T(8,128)S(1)} fusion(f32[8,512,1024]{2,1,0:T(8,128)} %get-tuple-element.101, f32[8,512]{1,0:T(8,128)S(1)} %get-tuple-element.100), kind=kLoop, calls=%fused_computation.17 | loop fusion | flops 12578816 | bytes 16809984 | tf_op jit(solution)/shard_map/while/body/eval_jaxpr/reduce_sum | solution.py:111
  133.6 6.0 %all-to-all-start.2 = ((f32[8,1,512]{2,1,0:T(1,128)}), f32[8,1,512]{2,1,0:T(1,128)S(1)}, u32[]{:S(2)}, u32[]{:S(2)}) async-start(f32[8,1,512]{2,1,0:T(1,128)} %reshape.99), calls=%async_computation.2 | async-start | bytes 32768 | tf_op jit(solution)/shard_map/all_to_all | solution.py:125
  139.6 8.2 %fusion.24 = f32[512,8,64]{0,2,1:T(8,128)} fusion(bf16[1024,8,64]{0,2,1:T(8,128)(2,1)S(1)} %reshape_reshape.3, f32[8,512,1024]{2,1,0:T(8,128)} %get-tuple-element.101, f32[8,512]{1,0:T(8,128)S(1)} %get-tuple-element.100), kind=kOutput, calls=%fused_computation.31 | convolution fusion | flops 549453824 | bytes 18890752 | tf_op jit(solution)/shard_map/while/body/eval_jaxpr/hqk,khd->qhd/dot_general | solution.py:113
  147.8 2.1 %copy.57 = f32[512,8,64]{2,1,0:T(8,128)S(1)} copy(f32[512,8,64]{0,2,1:T(8,128)} %fusion.24) | data formatting | bytes 2097152 | tf_op jit(solution)/shard_map/while/body/eval_jaxpr/hqk,khd->qhd/transpose | solution.py:113
  149.9 2.1 %reshape.95 = f32[8,1,32768]{2,1,0:T(1,128)} reshape(f32[512,8,64]{2,1,0:T(8,128)S(1)} %copy.57) | data formatting | bytes 2097152
  152.1 6.0 %all-to-all-start = ((f32[8,1,32768]{2,1,0:T(1,128)}), f32[8,1,32768]{2,1,0:T(1,128)S(1)}, u32[]{:S(2)}, u32[]{:S(2)}) async-start(f32[8,1,32768]{2,1,0:T(1,128)} %reshape.95), calls=%async_computation | async-start | bytes 2097152 | tf_op jit(solution)/shard_map/all_to_all | solution.py:123
  161.5 13.0 %all-to-all-done = f32[8,1,32768]{2,1,0:T(1,128)S(1)} async-done(((f32[8,1,32768]{2,1,0:T(1,128)}), f32[8,1,32768]{2,1,0:T(1,128)S(1)}, u32[]{:S(2)}, u32[]{:S(2)}) %all-to-all-start) | async-done | bytes 1048608 | tf_op jit(solution)/shard_map/all_to_all | solution.py:123
  174.4 3.1 %reduce.1 = f32[8,32768]{1,0:T(8,128)S(1)} reduce(f32[8,1,32768]{2,1,0:T(1,128)S(1)} %all-to-all-done, f32[]{:T(128)} %broadcast.73), dimensions={1}, to_apply=%all_to_all.15.reduce_sub_computation | reduce | bytes 2097156 | tf_op jit(solution)/shard_map/all_to_all | solution.py:123
  177.6 2.2 %reshape.96 = f32[512,8,64]{2,1,0:T(8,128)} reshape(f32[8,32768]{1,0:T(8,128)S(1)} %reduce.1) | data formatting | bytes 2097152
  179.8 2.4 %copy.60 = f32[8,64,8,64]{1,0,3,2:T(8,128)S(1)} copy(f32[8,64,8,64]{3,2,1,0:T(8,128)} %bitcast.63) | data formatting | bytes 2097152 | tf_op jit(solution)/shard_map/reshape | solution.py:128
  (74 shorter events, 28.7 us)
Async XLA Ops:
  5.6 44.4 %copy-start = (bf16[1024,512]{0,1:T(8,128)(2,1)}, bf16[1024,512]{0,1:T(8,128)(2,1)S(1)}, u32[]{:S(2)}) copy-start(bf16[1024,512]{0,1:T(8,128)(2,1)S(1)} %copy.56) | copy-start | bytes 3145732
  15.5 68.7 %collective-permute-start = (bf16[64,512]{0,1:T(8,128)(2,1)S(1)}, bf16[64,512]{0,1:T(8,128)(2,1)S(1)}, u32[]{:S(2)}, u32[]{:S(2)}) collective-permute-start(bf16[64,512]{0,1:T(8,128)(2,1)S(1)} %fusion.36), channel_id=1, source_target_pairs={{0,1},{1,0},{2,3},{3,2},{4,5},{5,4},{6,7},{7,6},{8,9},{9,8},{10,11... | collective-permute-start | bytes 196616 | tf_op jit(solution)/shard_map/ppermute | solution.py:16
  84.2 0.6 copy-start.5
  85.0 14.5 %collective-permute-start.1 = (bf16[128,512]{0,1:T(8,128)(2,1)S(1)}, bf16[128,512]{0,1:T(8,128)(2,1)S(1)}, u32[]{:S(2)}, u32[]{:S(2)}) collective-permute-start(bf16[128,512]{0,1:T(8,128)(2,1)S(1)} %maximum_select_fusion.5), channel_id=1, source_target_pairs={{0,2},{1,3},{2,0},{3,1},{4,6},{5,7},{6,4},{7,5},{8,10},{9,11},{10,... | collective-permute-start | bytes 393224 | tf_op jit(solution)/shard_map/ppermute | solution.py:16
  85.0 16.4 %copy-start.6 = (f32[512]{0:T(512)S(1)}, f32[512]{0:T(512)}, u32[]{:S(2)}) copy-start(f32[512]{0:T(512)} %param.21) | copy-start | bytes 6148
  86.6 2.7 %copy-start.4 = (bf16[512,8,64]{0,2,1:T(8,128)(2,1)S(1)}, bf16[512,8,64]{0,2,1:T(8,128)(2,1)}, u32[]{:S(2)}) copy-start(bf16[512,8,64]{0,2,1:T(8,128)(2,1)} %get-tuple-element.168) | copy-start | bytes 1572868 | tf_op jit(solution)/shard_map/while
  88.0 3.1 %copy-start.1 = (bf16[2,512,512]{1,2,0:T(8,128)(2,1)S(1)}, bf16[2,512,512]{1,2,0:T(8,128)(2,1)}, u32[]{:S(2)}) copy-start(bf16[2,512,512]{1,2,0:T(8,128)(2,1)} %get-tuple-element.157) | copy-start | bytes 3145732 | tf_op jit(solution)/shard_map/while
  91.3 1.0 copy-start.2
  93.8 2.7 %copy-start.4 = (bf16[512,8,64]{0,2,1:T(8,128)(2,1)S(1)}, bf16[512,8,64]{0,2,1:T(8,128)(2,1)}, u32[]{:S(2)}) copy-start(bf16[512,8,64]{0,2,1:T(8,128)(2,1)} %get-tuple-element.168) | copy-start | bytes 1572868 | tf_op jit(solution)/shard_map/while
  95.2 3.1 %copy-start.1 = (bf16[2,512,512]{1,2,0:T(8,128)(2,1)S(1)}, bf16[2,512,512]{1,2,0:T(8,128)(2,1)}, u32[]{:S(2)}) copy-start(bf16[2,512,512]{1,2,0:T(8,128)(2,1)} %get-tuple-element.157) | copy-start | bytes 3145732 | tf_op jit(solution)/shard_map/while
  98.5 1.0 copy-start.2
  100.3 10.4 %collective-permute-start.2 = (bf16[256,512]{0,1:T(8,128)(2,1)}, bf16[256,512]{0,1:T(8,128)(2,1)}, u32[]{:S(2)}, u32[]{:S(2)}) collective-permute-start(bf16[256,512]{0,1:T(8,128)(2,1)} %maximum_select_fusion.3), channel_id=1, source_target_pairs={{0,4},{1,5},{2,6},{3,7},{4,0},{5,1},{6,2},{7,3},{8,12},{9,13},{10,... | collective-permute-start | bytes 786440 | tf_op jit(solution)/shard_map/ppermute | solution.py:16
  120.6 13.0 %all-to-all-start.1 = ((f32[8,1,512]{2,1,0:T(1,128)}), f32[8,1,512]{2,1,0:T(1,128)S(1)}, u32[]{:S(2)}, u32[]{:S(2)}) async-start(f32[8,1,512]{2,1,0:T(1,128)} %reshape.97), calls=%async_computation.1 | async-start | bytes 32768 | tf_op jit(solution)/shard_map/all_to_all | solution.py:124
  133.6 18.4 %all-to-all-start.2 = ((f32[8,1,512]{2,1,0:T(1,128)}), f32[8,1,512]{2,1,0:T(1,128)S(1)}, u32[]{:S(2)}, u32[]{:S(2)}) async-start(f32[8,1,512]{2,1,0:T(1,128)} %reshape.99), calls=%async_computation.2 | async-start | bytes 32768 | tf_op jit(solution)/shard_map/all_to_all | solution.py:125
  147.8 10.3 %copy-start.3 = (bf16[2,512,512]{1,2,0:T(8,128)(2,1)S(1)}, bf16[2,512,512]{1,2,0:T(8,128)(2,1)}, u32[]{:S(2)}) copy-start(bf16[2,512,512]{1,2,0:T(8,128)(2,1)} %get-tuple-element.55) | copy-start | bytes 3145732
  152.1 22.4 %all-to-all-start = ((f32[8,1,32768]{2,1,0:T(1,128)}), f32[8,1,32768]{2,1,0:T(1,128)S(1)}, u32[]{:S(2)}, u32[]{:S(2)}) async-start(f32[8,1,32768]{2,1,0:T(1,128)} %reshape.95), calls=%async_computation | async-start | bytes 2097152 | tf_op jit(solution)/shard_map/all_to_all | solution.py:123
